TPU v7x, 512 devices: a whole 4x4x16 slice. The times are simulated.
512 devices in a mesh: dp: 2 (over core), ctx: 32 (over x, z_lo), tensor: 8 (over z_hi, y).
Axes of the slice: x: 4, y: 4, z: 16 (z_hi: 2, z_lo: 8; z = z_hi * 8 + z_lo), core: 2. Of those that a mesh axis runs over, the one named last changes fastest.
Arguments:
- tokens: bfloat16 [2, 4096, 2048], P('dp', 'ctx', 'tensor'), may hold values from -6 to 6
- cotangent: bfloat16 [2, 4096, 2048], P('dp', 'ctx', 'tensor'), may hold values from -6 to 6
- w_value: bfloat16 [2048, 2048], P('ctx', 'tensor'), may hold values from -0.125 to 0.125
- w_gate: bfloat16 [2048, 2048], P('ctx', 'tensor'), may hold values from -0.125 to 0.125
- decay_rate: float32 [4, 2048], P(None, 'tensor'), as said below
- residue: float32 [4, 2048], P(None, 'tensor'), may hold values from -4 to 4
- skip_gain: float32 [2048], P('tensor'), may hold values from -4 to 4
- contig_len: int32 [2, 8], P('dp'), may hold values from 1 to 1536, 4096 in all within a row
Outputs:
- output: bfloat16 [2, 4096, 2048], P('dp', 'ctx', 'tensor')
- grad_tokens: bfloat16 [2, 4096, 2048], P('dp', 'ctx', 'tensor')
- grad_w_value: float32 [2048, 2048], P('ctx', 'tensor')
- grad_w_gate: float32 [2048, 2048], P('ctx', 'tensor')
- grad_skip: float32 [2048], P('tensor')
- grad_residue: float32 [4, 2048], P(None, 'tensor')
- grad_rate: float32 [4, 2048], P(None, 'tensor')
Inputs may be any that keep to these rules, and one draw needn't show every extreme that they name: `contig_len`: each row's lengths sum to 4096; the largest of each row is exactly 1536. `decay_rate`: every rate lies between 0.25 / 4096 and 1 / 30.
All inputs are finite; a program needn't handle non-finite values.
Results may differ from a plain program's by a relative error of at most 0.012.
Values may be sent and summed in bfloat16 or wider, within the bound.
A program may use at most 64 MiB of HBM per device.

v0:
```python
import jax
import jax.numpy as jnp
from jax import lax
from jax.sharding import PartitionSpec as P


def carried_in(part, axis, combine, identity, reverse):
    count = lax.axis_size(axis)
    place = lax.axis_index(axis)
    ahead = count - 1 - place if reverse else place
    gathered = jax.tree.map(lambda a: lax.all_gather(a, axis), part)
    state = jax.tree.map(lambda a, e: jnp.zeros_like(a) + jnp.asarray(e, a.dtype), part, identity)

    def one(hop, state):
        source = count - 1 - hop if reverse else hop
        return combine(
            state, jax.tree.map(lambda a: lax.dynamic_index_in_dim(a, source, 0, False), gathered)
        )

    return lax.fori_loop(0, ahead, one, state)


def link(first, second):
    return (first[0] * second[0], second[0] * first[1] + second[1])


def body(tokens, cotangent, w_value, w_gate, decay_rate, residue, skip_gain, contig_len):
    rows, span, width = tokens.shape
    flat = tokens.reshape(rows * span, width)
    feats = lax.all_gather(flat, "tensor", axis=1, tiled=True)
    paired_w = jnp.concatenate([w_value, w_gate], axis=1)
    whole = lax.all_gather(paired_w, "ctx", axis=0, tiled=True)
    both = jnp.dot(feats, whole, preferred_element_type=jnp.float32)
    value = both[:, :width].reshape(rows, span, width)
    gate = both[:, width:].reshape(rows, span, width)
    me = lax.axis_index("ctx")
    first = me * span
    positions = first + jnp.arange(span, dtype=jnp.int32)
    starts = jnp.cumsum(contig_len, axis=1) - contig_len
    here = starts[:, None, :]
    place = positions[None, :, None]
    reset = jnp.any(place == here, axis=2).astype(jnp.float32)
    reset_next = jnp.any(place + 1 == here, axis=2).astype(jnp.float32)
    clear_fwd = jnp.all((here < first) | (here > place), axis=2).astype(jnp.float32)
    clear_back = jnp.all((here <= place) | (here > first + span), axis=2).astype(jnp.float32)
    pole = jnp.exp(-decay_rate)
    factor = jnp.sqrt(-jnp.expm1(-2.0 * decay_rate))
    weight_mode = residue * factor
    steps_in = (jnp.arange(span, dtype=jnp.int32) + 1).astype(jnp.float32)
    decay_fwd = jnp.exp(-decay_rate[None] * steps_in[:, None, None])
    decay_back = decay_fwd[::-1]
    keep = (1.0 - reset)[:, :, None, None] * pole
    drive = jnp.broadcast_to(value[:, :, None, :], keep.shape)
    local = lax.associative_scan(link, (keep, drive), axis=1)[1]
    scale_end = decay_fwd[-1][None] * clear_fwd[:, -1][:, None, None]
    end_state = local[:, -1]
    _, incoming = carried_in(
        (scale_end, end_state),
        "ctx",
        link,
        (jnp.ones_like(scale_end), jnp.zeros_like(end_state)),
        False,
    )
    state = local + decay_fwd[None] * clear_fwd[:, :, None, None] * incoming[:, None]
    mixed = jnp.sum(weight_mode * state, axis=2) + skip_gain * value
    output = (gate * mixed).astype(jnp.bfloat16)
    upstream = cotangent.astype(jnp.float32)
    grad_mixed = upstream * gate
    grad_gate = upstream * mixed
    keep_back = (1.0 - reset_next)[:, :, None, None] * pole
    source = grad_mixed[:, :, None, :] * weight_mode
    local_back = lax.associative_scan(link, (keep_back[:, ::-1], source[:, ::-1]), axis=1)[1][
        :, ::-1
    ]
    scale_top = decay_back[0][None] * clear_back[:, 0][:, None, None]
    top_state = local_back[:, 0]
    _, incoming_back = carried_in(
        (scale_top, top_state),
        "ctx",
        link,
        (jnp.ones_like(scale_top), jnp.zeros_like(top_state)),
        True,
    )
    grad_state = (
        local_back + decay_back[None] * clear_back[:, :, None, None] * incoming_back[:, None]
    )
    grad_value = jnp.sum(grad_state, axis=2) + skip_gain * grad_mixed
    skip_part = jnp.sum(grad_mixed * value, axis=(0, 1))
    paired_part = jnp.sum(grad_mixed[:, :, None, :] * state, axis=(0, 1))
    carried_part = jnp.sum(grad_state * (state - drive), axis=(0, 1))
    grad_skip, paired, carried = lax.psum((skip_part, paired_part, carried_part), ("dp", "ctx"))
    grad_residue = factor * paired
    grad_rate = -carried + residue * jnp.exp(-2.0 * decay_rate) / factor * paired
    cot_both = (
        jnp.concatenate([grad_value, grad_gate], axis=2)
        .astype(jnp.bfloat16)
        .reshape(rows * span, 2 * width)
    )
    contract = (((1,), (1,)), ((), ()))
    term = lax.dot_general(cot_both, whole, contract, preferred_element_type=jnp.float32)
    grad_tokens = lax.psum_scatter(
        term.astype(jnp.bfloat16), "tensor", scatter_dimension=1, tiled=True
    )
    grad_tokens = grad_tokens.reshape(rows, span, width)
    slabs = lax.all_to_all(feats, "ctx", split_axis=1, concat_axis=0, tiled=True)
    grad_w = lax.dot_general(
        slabs,
        lax.all_gather(cot_both, "ctx", axis=0, tiled=True),
        (((0,), (0,)), ((), ())),
        preferred_element_type=jnp.float32,
    )
    grad_w = lax.psum(grad_w, "dp")
    return (
        output,
        grad_tokens,
        grad_w[:, :width],
        grad_w[:, width:],
        grad_skip,
        grad_residue,
        grad_rate,
    )


def solution(mesh):
    in_specs = (
        P("dp", "ctx", "tensor"),
        P("dp", "ctx", "tensor"),
        P("ctx", "tensor"),
        P("ctx", "tensor"),
        P(None, "tensor"),
        P(None, "tensor"),
        P("tensor"),
        P("dp", None),
    )
    out_specs = (
        P("dp", "ctx", "tensor"),
        P("dp", "ctx", "tensor"),
        P("ctx", "tensor"),
        P("ctx", "tensor"),
        P("tensor"),
        P(None, "tensor"),
        P(None, "tensor"),
    )
    return jax.shard_map(body, mesh=mesh, in_specs=in_specs, out_specs=out_specs, check_vma=False)
```

profile of v0, /device:TPU:17, one launch (start us, length us, event | category | flops | bytes accessed | tf_op | source)
XLA Modules:
  0.0 1120.3 jit_solution(10773666285794444207)
XLA Ops:
  7.2 1.4 pad_maximum_fusion.5
  8.7 0.8 reduce_window_sum.11
  12.6 1.0 copy.23
  13.6 0.7 fusion.29
  14.7 0.7 slice.435
  16.0 117.6 %all-gather.2 = f32[32,4,256]{2,1,0:T(4,128)} all-gather(f32[1,4,256]{2,1,0:T(4,128)S(1)} %get-tuple-element.204), channel_id=4, replica_groups=mesh['dp'=2,'ctx'=32,'tensor'=8] {'ctx'}, dimensions={0}, use_global_device_ids=true | all-gather | bytes 135168 | tf_op jit(solution)/shard_map/all_gather | solution.py:11
  133.6 104.2 %all-gather.1 = f32[32,4,256]{2,1,0:T(4,128)} all-gather(f32[1,4,256]{2,1,0:T(4,128)S(1)} %get-tuple-element.205), channel_id=3, replica_groups=mesh['dp'=2,'ctx'=32,'tensor'=8] {'ctx'}, dimensions={0}, use_global_device_ids=true | all-gather | bytes 135168 | tf_op jit(solution)/shard_map/all_gather | solution.py:11
  237.8 53.8 %all-gather = bf16[1,128,2048]{1,2,0:T(8,128)(2,1)S(1)} all-gather(bf16[1,128,256]{1,2,0:T(8,128)(2,1)S(1)} %copy.23), channel_id=2, replica_groups=mesh['dp'=2,'ctx'=32,'tensor'=8] {'tensor'}, dimensions={2}, use_global_device_ids=true | all-gather | bytes 589824 | tf_op jit(solution)/shard_map/all_gather | solution.py:30
  291.7 2.1 convolution_bitcast_fusion
  296.5 0.8 slice.489
  298.9 0.7 pad_maximum_fusion.7
  301.4 0.8 pad.112
  302.2 0.8 pad.113
  303.8 1.0 slice_multiply_fusion
  306.9 0.7 pad_maximum_fusion.10
  307.8 0.7 pad_maximum_fusion.8
  308.7 0.7 pad_maximum_fusion.6
  309.9 0.7 fusion.9
  310.6 101.0 %all_gather.34 = f32[32,1,4,256]{3,2,1,0:T(4,128)S(1)} all-gather(f32[1,1,4,256]{3,2,1,0:T(4,128)} %slice_add_fusion.10), channel_id=1, replica_groups=mesh['dp'=2,'ctx'=32,'tensor'=8] {'ctx'}, dimensions={0}, use_global_device_ids=true | all-gather | bytes 135168 | tf_op jit(solution)/shard_map/all_gather | solution.py:11
  411.6 21.3 %while.27 = (s32[]{:T(128)}, f32[1,4,256]{2,1,0:T(4,128)S(1)}, s32[]{:T(128)}, f32[32,1,4,256]{3,2,1,0:T(4,128)}, f32[32,1,4,256]{3,2,1,0:T(4,128)S(1)}, /*index=5*/s32[]{:T(128)}, s32[]{:T(128)}, s32[]{:T(128)}, s32[]{:T(128)}) while((s32[]{:T(128)}, f32[1,4,256]{2,1,0:T(4,128)S(1)}, s32[]{:T(128)}, f32[32,1,4,256]{3,2,1,0:T(4,128)}, ...), condition=%wide.region_9.10_spmd, body=%wide.region_8.9_spmd.sunk | while | flops 2054 | bytes 16535 | solution.py:20
  413.7 0.7 bitcast_add_fusion.7
  414.4 0.7 bitcast_add_fusion.7
  415.8 0.7 bitcast_add_fusion.7
  418.5 0.7 bitcast_add_fusion.7
  419.2 0.7 bitcast_add_fusion.7
  420.6 0.7 bitcast_add_fusion.7
  421.9 0.7 bitcast_add_fusion.7
  422.6 0.7 bitcast_add_fusion.7
  424.0 0.7 bitcast_add_fusion.7
  424.7 0.7 bitcast_add_fusion.7
  426.1 0.7 bitcast_add_fusion.7
  427.5 0.7 bitcast_add_fusion.7
  428.1 0.7 bitcast_add_fusion.7
  429.5 0.7 bitcast_add_fusion.7
  431.6 0.7 bitcast_add_fusion.7
  433.0 0.9 pad_maximum_fusion.2
  434.7 0.8 add.297
  435.5 1.0 fusion.4
  437.2 0.8 pad.98
  438.1 22.1 %pad.99 = f32[1,128,4,256]{3,2,1,0:T(4,128)S(1)} pad(f32[1,64,4,256]{3,2,1,0:T(4,128)} %add.297, f32[]{:T(128)} %constant.69.clone.1), padding=0_0_0x1_0_1x0_0_0x0_0_0 | pad | bytes 786436 | tf_op jit(solution)/shard_map/pad | solution.py:54
  460.2 98.4 %all_gather.31 = f32[32,1,4,256]{3,2,1,0:T(4,128)S(1)} all-gather(f32[1,1,4,256]{3,2,1,0:T(4,128)S(1)} %slice_add_fusion.12), channel_id=1, replica_groups=mesh['dp'=2,'ctx'=32,'tensor'=8] {'ctx'}, dimensions={0}, use_global_device_ids=true | all-gather | bytes 135168 | tf_op jit(solution)/shard_map/all_gather | solution.py:11
  558.6 2.3 multiply_reduce_fusion
  561.8 44.6 %all_to_all.19 = bf16[128,32,64]{0,2,1:T(8,128)(2,1)S(1)} all-to-all(bf16[128,32,64]{0,2,1:T(8,128)(2,1)S(1)} %bitcast.93), channel_id=1, replica_groups=mesh['dp'=2,'ctx'=32,'tensor'=8] {'ctx'}, dimensions={1} | all-to-all | bytes 1048576 | tf_op jit(solution)/shard_map/all_to_all | solution.py:105
  606.4 246.9 %all-gather.8.cloned.1.call-done = bf16[4096,512]{1,0:T(8,128)(2,1)} async-done(((bf16[128,512]{1,0:T(8,128)(2,1)}), bf16[4096,512]{1,0:T(8,128)(2,1)}) %all-gather.8.cloned.1.call-update) | async-done | bytes 4194320 | tf_op jit(solution)/shard_map/all_gather | solution.py:108
  853.3 3.7 convolution_bitcast_fusion.1
  857.1 1.6 convolution_convert_fusion
  858.7 252.3 %all-reduce.28 = (f32[256]{0:T(256)}, f32[4,256]{1,0:T(4,128)S(1)}, f32[4,256]{1,0:T(4,128)S(1)}) all-reduce(f32[256]{0:T(256)S(1)} %get-tuple-element.210, f32[4,256]{1,0:T(4,128)S(1)} %get-tuple-element.169, f32[4,256]{1,0:T(4,128)S(1)} %get-tuple-element.167), channel_id=1, replica_groups=mesh['dp'=2,'ctx'=32,'tensor'=8] {'dp','ctx'}, use_global_device_ids=true, to_apply=%region_14.15 | all-reduce | flops 2304 | bytes 18432 | tf_op jit(solution)/shard_map/psum | solution.py:91
  1112.3 1.5 fusion.33
  (155 shorter events, 27.6 us)
Async XLA Ops:
  7.2 284.6 %all-gather.6.cloned.1.call-start = ((), (), s32[]{:S(2)}) async-start(), calls=%async_computation.2 | async-start | bytes 2162688 | tf_op jit(solution)/shard_map/all_gather | solution.py:32
  8.6 844.6 %all-gather.8.cloned.1.call-start = ((), (), s32[]{:S(2)}) async-start(), calls=%async_computation.4 | async-start | bytes 4325376 | tf_op jit(solution)/shard_map/all_gather | solution.py:108
  15.4 0.6 copy-start.10
  291.7 4.7 copy-start.5
  296.4 0.9 copy-start.2
  296.5 1.7 copy-start
  298.6 2.5 copy-start.3
  298.6 2.5 copy-start.4
  300.0 1.3 slice-start
  434.7 123.9 %copy-start.11 = (f32[128]{0:T(128)S(1)}, f32[128]{0:T(128)}, u32[]{:S(2)}) copy-start(f32[128]{0:T(128)} %copy-done.10) | copy-start | bytes 1540
  438.1 122.9 %copy-start.6 = (bf16[1,128,256]{2,1,0:T(8,128)(2,1)S(1)}, bf16[1,128,256]{2,1,0:T(8,128)(2,1)}, u32[]{:S(2)}) copy-start(bf16[1,128,256]{2,1,0:T(8,128)(2,1)} %param.13) | copy-start | bytes 196612
  438.1 122.9 %copy-start.9 = (f32[256]{0:T(256)S(1)}, f32[256]{0:T(256)}, u32[]{:S(2)}) copy-start(f32[256]{0:T(256)} %param.18) | copy-start | bytes 3076
  561.7 550.6 %all-reduce.31.cloned.1.call-start = ((), (), s32[]{:S(2)}) async-start(), calls=%async_computation.5 | async-start | bytes 262144 | tf_op jit(solution)/shard_map/psum | solution.py:112
  606.4 250.7 %copy-start.1 = (bf16[2048,512]{1,0:T(8,128)(2,1)S(1)}, bf16[2048,512]{1,0:T(8,128)(2,1)}, u32[]{:S(2)}) copy-start(bf16[2048,512]{1,0:T(8,128)(2,1)} %all-gather.6.cloned.1.call-done) | copy-start | bytes 6291460
  857.0 254.0 %copy-start.7 = (f32[4,256]{1,0:T(4,128)S(1)}, f32[4,256]{1,0:T(4,128)}, u32[]{:S(2)}) copy-start(f32[4,256]{1,0:T(4,128)} %param.17) | copy-start | bytes 12292
  857.0 254.0 %copy-start.8 = (f32[4,256]{1,0:T(4,128)S(1)}, f32[4,256]{1,0:T(4,128)}, u32[]{:S(2)}) copy-start(f32[4,256]{1,0:T(4,128)} %param.16) | copy-start | bytes 12292
  857.0 256.8 %reduce-scatter.2.cloned.1.call-start = ((), (), s32[]{:S(2)}) async-start(), calls=%async_computation.3 | async-start | bytes 589824 | tf_op jit(solution)/shard_map/reduce_scatter | solution.py:101
Sparse Core Ops, SparseCore 0:
  10.6 209.9 all-gather.5
  561.8 291.4 all-gather.7
  857.1 59.6 all-reduce.30
  921.7 110.2 reduce-scatter.1
where the time goes:
time: 1120 us
  blocking collectives  772 us (69%)
  waiting for transfers between devices  247 us (22%)
  other arithmetic  40.2 us (4%)
  local copies, waits for them, and re-layouts  38.6 us (3%)
  between operations  15 us (1%)
    all_gather x4, blocking collectives, carried_in(): gathered = jax.tree.map(lambda a: lax.all_gather(a, axis), part)  421 us
    psum x1, blocking collectives, body(): lax.psum((skip_part, paired_part, carried_part), ('dp', 'ctx'))  252 us
    all_gather x1, waiting for transfers between devices, body(): lax.all_gather(cot_both, 'ctx', axis=0, tiled=True)  247 us
    all_gather x1, blocking collectives, body(): feats = lax.all_gather(flat, 'tensor', axis=1, tiled=True)  53.8 us
    all_to_all x1, blocking collectives, body(): lax.all_to_all(feats, 'ctx', split_axis=1, concat_axis=0, tiled=True)  44.6 us
    pad x12, local copies, waits for them, and re-layouts, body(): local = lax.associative_scan(link, (keep, drive), axis=1)[1]  24.6 us
    add x42, other arithmetic, link(): return (first[0] * second[0], second[0] * first[1] + second[1])  23.3 us
  transfers between devices with their start and end apart: 4, of which 1 were waited for; matrix products, arithmetic and copies ran while one was open for 1% of the time, Pallas kernels for 0%

commit v1 on v0

--- a/solution.py
+++ b/solution.py
@@ -103,9 +103,21 @@
     )
     grad_tokens = grad_tokens.reshape(rows, span, width)
     slabs = lax.all_to_all(feats, "ctx", split_axis=1, concat_axis=0, tiled=True)
+
+    def _take_results(row_axis, xin):
+        return jnp.concatenate(
+            lax.all_to_all(
+                jnp.stack(lax.psum(1, axis_name=row_axis) * [xin], axis=0),
+                axis_name=row_axis,
+                split_axis=0,
+                concat_axis=0,
+            ),
+            0,
+        )
+
     grad_w = lax.dot_general(
         slabs,
-        lax.all_gather(cot_both, "ctx", axis=0, tiled=True),
+        _take_results("ctx", cot_both),
         (((0,), (0,)), ((), ())),
         preferred_element_type=jnp.float32,
     )

time: 1120 us -> 986 us (0.88)
  the two profiles are of different devices: /device:TPU:17 before, /device:TPU:25 now
where the time goes in v1:
time: 986 us; the launch traced here: 984 us
  blocking collectives  899 us (91%)
  other arithmetic  33.4 us (3%)
  local copies, waits for them, and re-layouts  17.4 us (2%)
  between operations  15.1 us (2%)
  starting transfers between devices  14 us (1%)
    all_gather x4, blocking collectives, carried_in(): gathered = jax.tree.map(lambda a: lax.all_gather(a, axis), part)  422 us
    psum x1, blocking collectives, body(): lax.psum((skip_part, paired_part, carried_part), ('dp', 'ctx'))  242 us
    all_to_all x1, blocking collectives, _take_results(): lax.all_to_all(jnp.stack(lax.psum(1, axis_name=row_axis) * [xin], axis=0)...  170 us
    all_gather x1, blocking collectives, body(): feats = lax.all_gather(flat, 'tensor', axis=1, tiled=True)  64.5 us
    add x42, other arithmetic, link(): return (first[0] * second[0], second[0] * first[1] + second[1])  22.9 us
  transfers between devices with their start and end apart: 4, of which 0 were waited for; matrix products, arithmetic and copies ran while one was open for 5% of the time, Pallas kernels for 0%

profile of v1, /device:TPU:25, one launch (start us, length us, event | category | flops | bytes accessed | tf_op | source)
XLA Modules:
  0.0 983.8 jit_solution(14726727241982091840)
XLA Ops:
  7.2 1.4 pad_maximum_fusion.5
  8.7 64.5 %all-gather = bf16[1,128,2048]{2,1,0:T(8,128)(2,1)S(1)} all-gather(bf16[1,128,256]{2,1,0:T(8,128)(2,1)} %param.12), channel_id=2, replica_groups=mesh['dp'=2,'ctx'=32,'tensor'=8] {'tensor'}, dimensions={2}, use_global_device_ids=true | all-gather | bytes 589824 | tf_op jit(solution)/shard_map/all_gather | solution.py:30
  73.2 1.0 copy.22
  74.2 13.8 %all-to-all-start.1 = ((bf16[128,32,64]{0,2,1:T(8,128)(2,1)}), bf16[128,32,64]{0,2,1:T(8,128)(2,1)S(1)}, u32[]{:S(2)}, u32[]{:S(2)}) async-start(bf16[128,32,64]{0,2,1:T(8,128)(2,1)} %bitcast.27), calls=%async_computation.2 | async-start | bytes 1048576 | tf_op jit(solution)/shard_map/all_to_all | solution.py:105
  91.2 0.7 slice.435
  92.4 114.6 %all-gather.2 = f32[32,4,256]{2,1,0:T(4,128)} all-gather(f32[1,4,256]{2,1,0:T(4,128)S(1)} %get-tuple-element.199), channel_id=4, replica_groups=mesh['dp'=2,'ctx'=32,'tensor'=8] {'ctx'}, dimensions={0}, use_global_device_ids=true | all-gather | bytes 135168 | tf_op jit(solution)/shard_map/all_gather | solution.py:11
  207.0 103.3 %all-gather.1 = f32[32,4,256]{2,1,0:T(4,128)} all-gather(f32[1,4,256]{2,1,0:T(4,128)S(1)} %get-tuple-element.200), channel_id=3, replica_groups=mesh['dp'=2,'ctx'=32,'tensor'=8] {'ctx'}, dimensions={0}, use_global_device_ids=true | all-gather | bytes 135168 | tf_op jit(solution)/shard_map/all_gather | solution.py:11
  310.4 2.0 convolution_bitcast_fusion
  315.1 0.8 slice.489
  318.7 0.8 pad.112
  319.5 0.8 pad.113
  320.5 1.0 slice_multiply_fusion
  323.7 0.7 pad_maximum_fusion.10
  324.5 0.7 pad_maximum_fusion.8
  325.5 0.7 pad_maximum_fusion.6
  326.7 104.7 %all_gather.31 = f32[32,1,4,256]{3,2,1,0:T(4,128)} all-gather(f32[1,1,4,256]{3,2,1,0:T(4,128)S(1)} %slice_add_fusion.10), channel_id=1, replica_groups=mesh['dp'=2,'ctx'=32,'tensor'=8] {'ctx'}, dimensions={0}, use_global_device_ids=true | all-gather | bytes 135168 | tf_op jit(solution)/shard_map/all_gather | solution.py:11
  432.4 1.0 fusion.3
  434.2 0.8 pad.98
  435.0 0.8 pad.99
  435.9 99.0 %all_gather.28 = f32[32,1,4,256]{3,2,1,0:T(4,128)S(1)} all-gather(f32[1,1,4,256]{3,2,1,0:T(4,128)S(1)} %slice_add_fusion.12), channel_id=1, replica_groups=mesh['dp'=2,'ctx'=32,'tensor'=8] {'ctx'}, dimensions={0}, use_global_device_ids=true | all-gather | bytes 135168 | tf_op jit(solution)/shard_map/all_gather | solution.py:11
  534.9 21.5 %while.27 = (s32[]{:T(128)}, f32[1,4,256]{2,1,0:T(4,128)S(1)}, s32[]{:T(128)}, f32[32,1,4,256]{3,2,1,0:T(4,128)}, f32[32,1,4,256]{3,2,1,0:T(4,128)}, /*index=5*/s32[]{:T(128)}, s32[]{:T(128)}, s32[]{:T(128)}, s32[]{:T(128)}) while((s32[]{:T(128)}, f32[1,4,256]{2,1,0:T(4,128)S(1)}, s32[]{:T(128)}, f32[32,1,4,256]{3,2,1,0:T(4,128)}, ...), condition=%wide.region_9.10_spmd, body=%wide.region_8.9_spmd.sunk | while | flops 2054 | bytes 16535 | solution.py:20
  534.9 0.7 bitcast_add_fusion.7
  535.6 0.7 bitcast_add_fusion.7
  536.3 0.7 bitcast_add_fusion.7
  537.0 0.7 bitcast_add_fusion.7
  537.7 0.7 bitcast_add_fusion.7
  538.4 0.7 bitcast_add_fusion.7
  541.8 0.7 bitcast_add_fusion.7
  542.5 0.7 bitcast_add_fusion.7
  543.9 0.7 bitcast_add_fusion.7
  544.6 0.7 bitcast_add_fusion.7
  545.3 0.7 bitcast_add_fusion.7
  546.0 0.7 bitcast_add_fusion.7
  546.7 0.7 bitcast_add_fusion.7
  548.7 0.7 bitcast_add_fusion.7
  549.4 0.7 bitcast_add_fusion.7
  551.5 0.7 bitcast_add_fusion.7
  552.2 0.7 bitcast_add_fusion.7
  552.9 0.7 bitcast_add_fusion.7
  553.6 0.7 bitcast_add_fusion.7
  554.3 0.7 bitcast_add_fusion.7
  555.7 0.7 bitcast_add_fusion.7
  556.4 1.4 multiply_reduce_fusion
  558.5 170.3 %all_to_all.21 = bf16[32,128,512]{2,1,0:T(8,128)(2,1)S(1)} all-to-all(bf16[32,128,512]{2,1,0:T(8,128)(2,1)S(1)} %stack.3), channel_id=1, replica_groups=mesh['dp'=2,'ctx'=32,'tensor'=8] {'ctx'}, dimensions={0} | all-to-all | bytes 8388608 | tf_op jit(solution)/shard_map/all_to_all | solution.py:109
  728.8 1.5 convolution_bitcast_fusion.1
  730.4 1.6 convolution_convert_fusion
  732.0 242.4 %all-reduce.28 = (f32[256]{0:T(256)}, f32[4,256]{1,0:T(4,128)S(1)}, f32[4,256]{1,0:T(4,128)S(1)}) all-reduce(f32[256]{0:T(256)S(1)} %get-tuple-element.205, f32[4,256]{1,0:T(4,128)S(1)} %get-tuple-element.164, f32[4,256]{1,0:T(4,128)S(1)} %get-tuple-element.162), channel_id=1, replica_groups=mesh['dp'=2,'ctx'=32,'tensor'=8] {'dp','ctx'}, use_global_device_ids=true, to_apply=%region_14.15 | all-reduce | flops 2304 | bytes 18432 | tf_op jit(solution)/shard_map/psum | solution.py:91
  975.7 1.5 fusion.32
  (173 shorter events, 22.0 us)
Async XLA Ops:
  7.2 80.9 %copy-start.18 = (s32[1,8]{1,0:T(1,128)S(1)}, s32[1,8]{1,0:T(1,128)}, u32[]{:S(2)}) copy-start(s32[1,8]{1,0:T(1,128)} %param.19) | copy-start | bytes 100
  7.2 83.6 %copy-start.10 = (f32[4,256]{1,0:T(4,128)S(1)}, f32[4,256]{1,0:T(4,128)}, u32[]{:S(2)}) copy-start(f32[4,256]{1,0:T(4,128)} %param.17) | copy-start | bytes 12292
  7.2 83.6 %copy-start.12 = (f32[4,256]{1,0:T(4,128)S(1)}, f32[4,256]{1,0:T(4,128)}, u32[]{:S(2)}) copy-start(f32[4,256]{1,0:T(4,128)} %param.16) | copy-start | bytes 12292
  7.2 303.2 %all-gather.5.cloned.1.call-start = ((), (), s32[]{:S(2)}) async-start(), calls=%async_computation.3 | async-start | bytes 2162688 | tf_op jit(solution)/shard_map/all_gather | solution.py:32
  74.2 483.8 %all-to-all-start.1 = ((bf16[128,32,64]{0,2,1:T(8,128)(2,1)}), bf16[128,32,64]{0,2,1:T(8,128)(2,1)S(1)}, u32[]{:S(2)}, u32[]{:S(2)}) async-start(bf16[128,32,64]{0,2,1:T(8,128)(2,1)} %bitcast.27), calls=%async_computation.2 | async-start | bytes 1048576 | tf_op jit(solution)/shard_map/all_to_all | solution.py:105
  88.0 887.7 %all-reduce.31.cloned.1.call-start = ((), (), s32[]{:S(2)}) async-start(), calls=%async_computation.5 | async-start | bytes 262144 | tf_op jit(solution)/shard_map/psum | solution.py:124
  91.9 0.6 copy-start.16
  310.3 4.6 copy-start.8
  315.0 0.9 copy-start.2
  315.1 1.1 copy-start.1
  316.6 1.9 copy-start.6
  316.6 1.9 copy-start.7
  317.4 1.3 slice-start
  432.4 124.0 %copy-start.3 = (f32[128,256]{1,0:T(8,128)S(1)}, f32[128,256]{1,0:T(8,128)}, u32[]{:S(2)}) copy-start(f32[128,256]{1,0:T(8,128)} %copy-done.2) | copy-start | bytes 393220
  432.4 124.0 %copy-start.17 = (f32[128]{0:T(128)S(1)}, f32[128]{0:T(128)}, u32[]{:S(2)}) copy-start(f32[128]{0:T(128)} %copy-done.16) | copy-start | bytes 1540
  432.4 124.0 %copy-start.19 = (f32[128]{0:T(128)S(1)}, f32[128]{0:T(128)}, u32[]{:S(2)}) copy-start(f32[128]{0:T(128)} %convert_element_type.88) | copy-start | bytes 1540
  432.4 124.0 %copy-start.20 = (f32[128]{0:T(128)S(1)}, f32[128]{0:T(128)}, u32[]{:S(2)}) copy-start(f32[128]{0:T(128)} %convert_element_type.82) | copy-start | bytes 1540
  435.0 122.8 %copy-start.9 = (bf16[1,128,256]{2,1,0:T(8,128)(2,1)S(1)}, bf16[1,128,256]{2,1,0:T(8,128)(2,1)}, u32[]{:S(2)}) copy-start(bf16[1,128,256]{2,1,0:T(8,128)(2,1)} %param.13) | copy-start | bytes 196612
  435.0 122.8 %copy-start.14 = (f32[256]{0:T(256)S(1)}, f32[256]{0:T(256)}, u32[]{:S(2)}) copy-start(f32[256]{0:T(256)} %param.18) | copy-start | bytes 3076
  557.8 0.7 copy-start.4
  728.8 1.6 copy-start
  730.3 244.1 %copy-start.11 = (f32[4,256]{1,0:T(4,128)S(1)}, f32[4,256]{1,0:T(4,128)}, u32[]{:S(2)}) copy-start(f32[4,256]{1,0:T(4,128)} %param.17) | copy-start | bytes 12292
  730.3 244.1 %copy-start.13 = (f32[4,256]{1,0:T(4,128)S(1)}, f32[4,256]{1,0:T(4,128)}, u32[]{:S(2)}) copy-start(f32[4,256]{1,0:T(4,128)} %param.16) | copy-start | bytes 12292
  730.3 244.8 %copy-start.5 = (f32[128,256]{1,0:T(8,128)S(1)}, f32[128,256]{1,0:T(8,128)}, u32[]{:S(2)}) copy-start(f32[128,256]{1,0:T(8,128)} %copy-done.4) | copy-start | bytes 393220
  730.3 244.8 %copy-start.15 = (f32[256]{0:T(256)S(1)}, f32[256]{0:T(256)}, u32[]{:S(2)}) copy-start(f32[256]{0:T(256)} %param.18) | copy-start | bytes 3076
  730.3 246.9 %reduce-scatter.2.cloned.1.call-start = ((), (), s32[]{:S(2)}) async-start(), calls=%async_computation.4 | async-start | bytes 589824 | tf_op jit(solution)/shard_map/reduce_scatter | solution.py:101
Sparse Core Ops, SparseCore 0:
  10.7 215.2 all-gather.4
  730.4 53.1 all-reduce.30
  788.7 112.0 reduce-scatter.1
